TPU v7x, 256 devices: a whole 4x4x8 slice. The times are simulated.
256 devices in a mesh: row: 8 (over x, core), col: 32 (over y, z).
Axes of the slice: x: 4, y: 4, z: 8, core: 2. Of those that a mesh axis runs over, the one named last changes fastest.
Arguments:
- affinity_tiles: bfloat16 [1024, 64, 128, 128], P(('row', 'col'))
- block_columns: int32 [1024, 64], P(('row', 'col')), may hold values from 0 to 127, as said below
- live_counts: int32 [8, 128], P('row', 'col'), may hold values from 1 to 64, 4096 in all within a row
- earlier_blocks: float32 [4, 64, 131072], P(None, None, ('row', 'col')), may hold values from -6 to 6
Outputs:
- new_blocks: float32 [2, 64, 131072], P(None, None, ('row', 'col'))
- triangular_factors: float32 [2, 64, 64], replicated
Inputs may be any that keep to these rules, and one draw needn't show every extreme that they name: `block_columns`: slot 0 of every block row names the block row itself; columns name block rows of the same row group. `live_counts`: slots at or past a block row's count are ignored.
All inputs are finite; a program needn't handle non-finite values.
Results may differ from a plain program's by a relative error of at most 0.0059.
Values may be sent and summed in bfloat16 or wider, within the bound.
No kernel may reach another device: no remote copies, remote signals or barrier semaphores. Data moves between devices by JAX's collectives and lax.ppermute only.
A program may use at most 64 MiB of HBM per device.

v0:
```python
import jax
import jax.numpy as jnp
from jax import lax
from jax.sharding import PartitionSpec as P

STEPS = 2


def apply_tiles(affinity_tiles, block_columns, row_counts, group_blocks):
    block_rows = affinity_tiles.shape[0]
    slot_count = affinity_tiles.shape[1]
    tile_size = affinity_tiles.shape[2]
    block_width = group_blocks.shape[0]
    slot_ids = lax.broadcasted_iota(jnp.int32, (block_rows, slot_count), 1)
    live_mask = slot_ids < row_counts[:, None]
    picked = jnp.take(group_blocks, block_columns, axis=1)
    picked = jnp.where(live_mask[None, :, :, None], picked, jnp.zeros((), jnp.bfloat16))
    running = jnp.einsum(
        "rsij,brsj->bri", affinity_tiles, picked, preferred_element_type=jnp.float32
    )
    return running.reshape(block_width, block_rows * tile_size)


def on_device(affinity_tiles, block_columns, live_counts, earlier_blocks):
    block_rows = affinity_tiles.shape[0]
    tile_size = affinity_tiles.shape[2]
    block_width = earlier_blocks.shape[1]
    rows_here = earlier_blocks.shape[2]
    total_rows = rows_here * lax.axis_size("row") * lax.axis_size("col")
    row_counts = live_counts.reshape(block_rows)
    known_list = [earlier_blocks[i] for i in range(earlier_blocks.shape[0])]
    first_half = known_list[-1].astype(jnp.bfloat16)
    group_half = lax.all_gather(first_half, "col", axis=1, tiled=True)
    fresh_list = []
    factor_list = []
    for step_index in range(STEPS):
        is_last = step_index + 1 == STEPS
        group_blocks = group_half.reshape(block_width, -1, tile_size)
        product = apply_tiles(affinity_tiles, block_columns, row_counts, group_blocks)
        known = jnp.concatenate(known_list, 0)
        local_proj = jnp.dot(known, product.T, precision=lax.Precision.HIGHEST) / total_rows
        projections = lax.psum(local_proj, ("row", "col"))
        residual = product - jnp.dot(projections.T, known, precision=lax.Precision.HIGHEST)
        local_gram = jnp.dot(residual, residual.T, precision=lax.Precision.HIGHEST) / total_rows
        gram_sum = lax.psum(local_gram, ("row", "col"))
        factor_low = jnp.linalg.cholesky(gram_sum)
        fresh = jax.scipy.linalg.solve_triangular(factor_low, residual, lower=True)
        fresh_list.append(fresh)
        factor_list.append(factor_low.T)
        known_list.append(fresh)
        if not is_last:
            group_half = lax.all_gather(fresh.astype(jnp.bfloat16), "col", axis=1, tiled=True)
    return (jnp.stack(fresh_list), jnp.stack(factor_list))


def solution(mesh):
    return jax.shard_map(
        on_device,
        mesh=mesh,
        in_specs=(
            P(("row", "col"), None, None, None),
            P(("row", "col"), None),
            P("row", "col"),
            P(None, None, ("row", "col")),
        ),
        out_specs=(P(None, None, ("row", "col")), P()),
        check_vma=False,
    )
```

profile of v0, /device:TPU:1, one launch (start us, length us, event | category | flops | bytes accessed | tf_op | source)
XLA Modules:
  0.0 864.7 jit_solution(17645085274301516106)
XLA Ops:
  7.2 0.0 all-gather.3.cloned.1.call-start
  7.2 1.5 fusion.32
  8.8 0.0 all-gather.3.cloned.1.call-update
  8.8 0.0 all-reduce.3.cloned.1.call-start
  8.8 0.7 compare_select_fusion
  9.5 0.1 reshape.73
  9.6 0.8 iota_compare_fusion.2
  10.4 0.9 constant_dynamic-update-slice_fusion.4
  11.3 0.9 constant_dynamic-update-slice_fusion.3
  12.2 0.9 constant_dynamic-update-slice_fusion.2
  13.1 1.1 slice_bitcast_fusion.2
  14.3 71.6 %all-gather.3.cloned.1.call-done = bf16[64,16384]{1,0:T(8,128)(2,1)} async-done(((bf16[64,512]{1,0:T(8,128)(2,1)}), bf16[64,16384]{1,0:T(8,128)(2,1)}) %all-gather.3.cloned.1.call-update) | async-done | bytes 2097168 | tf_op jit(solution)/shard_map/all_gather | solution.py:33
  85.9 2.2 copy_bitcast_fusion.1
  88.1 3.0 gather_fusion
  91.1 6.3 fusion.12
  97.3 1.2 convolution_multiply_fusion.1
  98.6 0.0 all-reduce.3.cloned.1.call-update
  98.6 0.0 all-gather.5.cloned.1.call-start
  98.6 0.9 constant_dynamic-update-slice_fusion.1
  99.6 246.5 %all-reduce.3.cloned.1.call-done = f32[256,64]{1,0:T(8,128)} async-done(((f32[256,64]{1,0:T(8,128)}), f32[256,64]{1,0:T(8,128)}) %all-reduce.3.cloned.1.call-update) | async-done | bytes 65552 | tf_op jit(solution)/shard_map/psum | solution.py:42
  346.0 1.3 convolution_subtract_fusion.1
  347.3 0.3 convolution_multiply_fusion.3
  347.6 76.2 %psum.29 = f32[64,64]{0,1:T(8,128)S(1)} all-reduce(f32[64,64]{0,1:T(8,128)S(1)} %convolution_multiply_fusion.3), channel_id=1, replica_groups=mesh['row'=8,'col'=32] {'row','col'}, use_global_device_ids=true, to_apply=%region_1.3 | all-reduce | flops 4096 | bytes 32768 | tf_op jit(solution)/shard_map/psum | solution.py:45
  423.8 0.1 copy.16
  423.9 5.8 cholesky.44
  429.8 0.6 compare_reduce_fusion.1
  430.4 0.7 fusion.24
  431.1 4.9 custom-call.6
  436.0 1.0 fusion.33
  437.0 0.0 all-gather.5.cloned.1.call-update
  437.0 0.0 all-reduce.5.cloned.1.call-start
  437.0 66.8 %all-gather.5.cloned.1.call-done = bf16[64,16384]{1,0:T(8,128)(2,1)} async-done(((bf16[64,512]{1,0:T(8,128)(2,1)}), bf16[64,16384]{1,0:T(8,128)(2,1)}) %all-gather.5.cloned.1.call-update) | async-done | bytes 2097168 | tf_op jit(solution)/shard_map/all_gather | solution.py:52
  503.8 2.2 copy_bitcast_fusion
  506.0 3.0 gather_fusion.1
  509.0 6.3 fusion.13
  515.3 1.3 convolution_multiply_fusion
  516.7 251.0 %all-reduce.5.cloned.1.call-done = f32[320,64]{1,0:T(8,128)} async-done(((f32[320,64]{1,0:T(8,128)}), f32[320,64]{1,0:T(8,128)}) %all-reduce.5.cloned.1.call-update) | async-done | bytes 81936 | tf_op jit(solution)/shard_map/psum | solution.py:42
  767.7 1.5 convolution_subtract_fusion
  769.2 0.3 convolution_multiply_fusion.2
  769.4 74.8 %psum.31 = f32[64,64]{0,1:T(8,128)S(1)} all-reduce(f32[64,64]{0,1:T(8,128)S(1)} %convolution_multiply_fusion.2), channel_id=1, replica_groups=mesh['row'=8,'col'=32] {'row','col'}, use_global_device_ids=true, to_apply=%region_5.9 | all-reduce | flops 4096 | bytes 32768 | tf_op jit(solution)/shard_map/psum | solution.py:45
  844.2 0.1 copy.20
  844.3 5.8 cholesky.55
  850.2 0.6 compare_reduce_fusion
  850.8 0.7 fusion.25
  851.5 0.7 copy.21
  852.2 4.9 custom-call.7
  857.1 0.3 convolution_bitcast_fusion
  857.4 0.7 pad_maximum_fusion.3
  (7 shorter events, 0.1 us)
Async XLA Ops:
  7.2 78.7 %all-gather.3.cloned.1.call-start = ((), (), s32[]{:S(2)}) async-start(), calls=%async_computation | async-start | bytes 2162688 | tf_op jit(solution)/shard_map/all_gather | solution.py:33
  8.8 337.2 %all-reduce.3.cloned.1.call-start = ((), (), s32[]{:S(2)}) async-start(), calls=%async_computation.1 | async-start | bytes 262144 | tf_op jit(solution)/shard_map/psum | solution.py:42
  98.6 405.2 %all-gather.5.cloned.1.call-start = ((), (), s32[]{:S(2)}) async-start(), calls=%async_computation.2 | async-start | bytes 2162688 | tf_op jit(solution)/shard_map/all_gather | solution.py:52
  437.0 330.7 %all-reduce.5.cloned.1.call-start = ((), (), s32[]{:S(2)}) async-start(), calls=%async_computation.3 | async-start | bytes 327680 | tf_op jit(solution)/shard_map/psum | solution.py:42
Sparse Core Ops, SparseCore 0:
  11.0 74.8 all-gather.2
  98.7 247.2 all-reduce.2
  437.1 66.6 all-gather.4
  516.8 250.8 all-reduce.4
where the time goes:
time: 865 us
  waiting for transfers between devices  636 us (74%)
  blocking collectives  151 us (17%)
  other arithmetic  26.4 us (3%)
  matrix products  19.7 us (2%)
  local copies, waits for them, and re-layouts  17.7 us (2%)
  between operations  13.9 us (2%)
    psum x2, waiting for transfers between devices, on_device(): projections = lax.psum(local_proj, ('row', 'col'))  497 us
    psum x2, blocking collectives, on_device(): gram_sum = lax.psum(local_gram, ('row', 'col'))  151 us
    all_gather x1, waiting for transfers between devices, on_device(): group_half = lax.all_gather(first_half, 'col', axis=1, tiled=True)  71.6 us
    all_gather x1, waiting for transfers between devices, on_device(): lax.all_gather(fresh.astype(jnp.bfloat16), 'col', axis=1, tiled=True)  66.8 us
  transfers between devices with their start and end apart: 4, of which 4 were waited for; matrix products, arithmetic and copies ran while one was open for 1% of the time, Pallas kernels for 0%

commit v1 on v0

--- a/solution.py
+++ b/solution.py
@@ -39,7 +39,7 @@
         product = apply_tiles(affinity_tiles, block_columns, row_counts, group_blocks)
         known = jnp.concatenate(known_list, 0)
         local_proj = jnp.dot(known, product.T, precision=lax.Precision.HIGHEST) / total_rows
-        projections = lax.psum(local_proj, ("row", "col"))
+        projections = jnp.sum(lax.all_gather(local_proj, ("row", "col")), axis=0)
         residual = product - jnp.dot(projections.T, known, precision=lax.Precision.HIGHEST)
         local_gram = jnp.dot(residual, residual.T, precision=lax.Precision.HIGHEST) / total_rows
         gram_sum = lax.psum(local_gram, ("row", "col"))

time: 865 us -> 672 us (0.78)
  waiting for transfers between devices: 636 us -> 413 us
  other arithmetic: 26.4 us -> 43.3 us
  local copies, waits for them, and re-layouts: 17.7 us -> 29.9 us
    psum x2 -> x0, waiting for transfers between devices: 497 us -> none  [on_device(): projections = lax.psum(local_proj, ('row', 'col'))]
    all_gather x0 -> x2, waiting for transfers between devices: none -> 272 us  [on_device(): projections = jnp.sum(lax.all_gather(local_proj, ('row', 'col')), axis=0)]
    reduce_sum x0 -> x2, other arithmetic: none -> 17 us  [on_device(): projections = jnp.sum(lax.all_gather(local_proj, ('row', 'col')), axis=0)]
    unnamed x5 -> x8, local copies, waits for them, and re-layouts: 4.38 us -> 16.6 us
  transfers between devices with their start and end apart: 4 -> 4, of which waited for: 4 -> 4; matrix products, arithmetic and copies ran while one was open for 1% -> 0% of each run, Pallas kernels for 0% -> 0%
where the time goes in v1:
time: 672 us; the launch traced here: 671 us
  waiting for transfers between devices  413 us (61%)
  blocking collectives  153 us (23%)
  other arithmetic  43.3 us (6%)
  local copies, waits for them, and re-layouts  29.9 us (4%)
  matrix products  18 us (3%)
  between operations  13.9 us (2%)
    all_gather x2, waiting for transfers between devices, on_device(): projections = jnp.sum(lax.all_gather(local_proj, ('row', 'col')), axis=0)  272 us
    psum x2, blocking collectives, on_device(): gram_sum = lax.psum(local_gram, ('row', 'col'))  153 us
    all_gather x1, waiting for transfers between devices, on_device(): group_half = lax.all_gather(first_half, 'col', axis=1, tiled=True)  74.4 us
    all_gather x1, waiting for transfers between devices, on_device(): lax.all_gather(fresh.astype(jnp.bfloat16), 'col', axis=1, tiled=True)  66.3 us
    reduce_sum x2, other arithmetic, on_device(): projections = jnp.sum(lax.all_gather(local_proj, ('row', 'col')), axis=0)  17 us
    unnamed x8, local copies, waits for them, and re-layouts  16.6 us
  transfers between devices with their start and end apart: 4, of which 4 were waited for; matrix products, arithmetic and copies ran while one was open for 0% of the time, Pallas kernels for 0%

profile of v1, /device:TPU:1, one launch (start us, length us, event | category | flops | bytes accessed | tf_op | source)
XLA Modules:
  0.0 671.3 jit_solution(1902080720864810698)
XLA Ops:
  7.2 0.0 all-gather.8.cloned.1.call-start
  7.2 1.5 fusion.33
  8.8 0.0 all-gather.8.cloned.1.call-update
  8.8 0.0 all-gather.12.cloned.1.call-start
  8.8 0.7 compare_select_fusion
  9.5 0.1 reshape.78
  9.6 0.8 iota_compare_fusion.2
  10.4 1.1 slice_bitcast_fusion.2
  11.5 74.4 %all-gather.8.cloned.1.call-done = bf16[64,16384]{1,0:T(8,128)(2,1)} async-done(((bf16[64,512]{1,0:T(8,128)(2,1)}), bf16[64,16384]{1,0:T(8,128)(2,1)}) %all-gather.8.cloned.1.call-update) | async-done | bytes 2097168 | tf_op jit(solution)/shard_map/all_gather | solution.py:33
  85.9 2.2 copy_bitcast_fusion.1
  88.1 3.0 gather_fusion
  91.1 6.3 fusion.12
  97.4 1.2 convolution_multiply_fusion.1
  98.6 0.0 all-gather.12.cloned.1.call-update
  98.7 0.0 all-gather.10.cloned.1.call-start
  98.8 131.4 %all-gather.12.cloned.1.call-done = f32[65536,64]{0,1:T(8,128)} async-done(((f32[256,64]{0,1:T(8,128)}), f32[65536,64]{0,1:T(8,128)}) %all-gather.12.cloned.1.call-update) | async-done | bytes 16777232 | tf_op jit(solution)/shard_map/all_gather | solution.py:42
  230.2 15.8 %copy.39 = f32[8,8,256,256]{3,2,1,0:T(8,128)} copy(f32[8,8,256,256]{3,1,2,0:T(8,128)} %bitcast.111) | data formatting | bytes 33554432
  246.1 7.5 %bitcast_reduce_fusion = f32[256,64]{0,1:T(8,128)S(1)} fusion(f32[8,8,256,256]{3,2,1,0:T(8,128)} %copy.39), kind=kLoop, calls=%fused_computation.2 | loop fusion | flops 4177920 | bytes 16842752 | tf_op jit(solution)/shard_map/reduce_sum | solution.py:42
  253.6 0.4 convolution_subtract_fusion.1
  254.0 0.3 convolution_multiply_fusion.3
  254.3 78.2 %psum.14 = f32[64,64]{0,1:T(8,128)S(1)} all-reduce(f32[64,64]{0,1:T(8,128)S(1)} %convolution_multiply_fusion.3), channel_id=1, replica_groups=mesh['row'=8,'col'=32] {'row','col'}, use_global_device_ids=true, to_apply=%region_1.3 | all-reduce | flops 4096 | bytes 32768 | tf_op jit(solution)/shard_map/psum | solution.py:45
  332.4 0.1 copy.25
  332.5 5.8 cholesky.44
  338.4 0.6 compare_reduce_fusion.1
  339.1 0.7 fusion.25
  339.7 4.9 custom-call.6
  344.6 1.0 fusion.34
  345.6 0.0 all-gather.10.cloned.1.call-update
  345.6 0.2 all-gather.14.cloned.1.call-start
  345.9 66.3 %all-gather.10.cloned.1.call-done = bf16[64,16384]{1,0:T(8,128)(2,1)} async-done(((bf16[64,512]{1,0:T(8,128)(2,1)}), bf16[64,16384]{1,0:T(8,128)(2,1)}) %all-gather.10.cloned.1.call-update) | async-done | bytes 2097168 | tf_op jit(solution)/shard_map/all_gather | solution.py:52
  412.1 2.2 copy_bitcast_fusion
  414.3 3.0 gather_fusion.1
  417.3 6.3 fusion.13
  423.6 1.4 fusion.14
  424.9 0.0 all-gather.14.cloned.1.call-update
  425.0 140.9 %all-gather.14.cloned.1.call-done = f32[256,320,64]{1,2,0:T(8,128)} async-done(((f32[1,320,64]{1,2,0:T(8,128)}), f32[256,320,64]{1,2,0:T(8,128)}) %all-gather.14.cloned.1.call-update) | async-done | bytes 20971536 | tf_op jit(solution)/shard_map/all_gather | solution.py:42
  565.8 9.5 %reduce_sum.19 = f32[320,64]{0,1:T(8,128)S(1)} reduce(f32[256,320,64]{1,2,0:T(8,128)} %all-gather.14.cloned.1.call-done, f32[]{:T(128)} %constant.52.clone.1), dimensions={0}, to_apply=%region_4.8 | reduce | flops 5222400 | bytes 21053444 | tf_op jit(solution)/shard_map/reduce_sum | solution.py:42
  575.3 0.6 convolution_subtract_fusion
  575.9 0.3 convolution_multiply_fusion.2
  576.1 74.7 %psum.15 = f32[64,64]{0,1:T(8,128)S(1)} all-reduce(f32[64,64]{0,1:T(8,128)S(1)} %convolution_multiply_fusion.2), channel_id=1, replica_groups=mesh['row'=8,'col'=32] {'row','col'}, use_global_device_ids=true, to_apply=%region_5.9 | all-reduce | flops 4096 | bytes 32768 | tf_op jit(solution)/shard_map/psum | solution.py:45
  650.8 0.1 copy.29
  650.9 5.8 cholesky.55
  656.8 0.6 compare_reduce_fusion
  657.5 0.7 fusion.26
  658.1 0.7 copy.30
  658.8 4.9 custom-call.7
  663.7 0.3 convolution_bitcast_fusion
  664.1 0.7 pad_maximum_fusion.3
  (12 shorter events, 0.1 us)
Async XLA Ops:
  7.2 78.7 %all-gather.8.cloned.1.call-start = ((), (), s32[]{:S(2)}) async-start(), calls=%async_computation | async-start | bytes 2162688 | tf_op jit(solution)/shard_map/all_gather | solution.py:33
  8.8 221.5 %all-gather.12.cloned.1.call-start = ((), (), s32[]{:S(2)}) async-start(), calls=%async_computation.2 | async-start | bytes 16842752 | tf_op jit(solution)/shard_map/all_gather | solution.py:42
  91.1 7.6 %copy-start = (f32[4,64,512]{2,1,0:T(8,128)S(1)}, f32[4,64,512]{2,1,0:T(8,128)}, u32[]{:S(2)}) copy-start(f32[4,64,512]{2,1,0:T(8,128)} %param.12) | copy-start | bytes 1572868
  98.7 313.4 %all-gather.10.cloned.1.call-start = ((), (), s32[]{:S(2)}) async-start(), calls=%async_computation.1 | async-start | bytes 2162688 | tf_op jit(solution)/shard_map/all_gather | solution.py:52
  345.6 220.2 %all-gather.14.cloned.1.call-start = ((), (), s32[]{:S(2)}) async-start(), calls=%async_computation.3 | async-start | bytes 25264128 | tf_op jit(solution)/shard_map/all_gather | solution.py:42
Sparse Core Ops, SparseCore 0:
  11.0 74.8 all-gather.7
  98.8 131.4 all-gather.11
  345.7 66.3 all-gather.9
  425.1 140.7 all-gather.13
